TPU v7x, 512 devices: a whole 4x4x16 slice. The times are simulated.
512 devices in a mesh: dp: 8 (over y, core), ctx: 64 (over z, x).
Axes of the slice: x: 4, y: 4, z: 16, core: 2. Of those that a mesh axis runs over, the one named last changes fastest.
Arguments:
- queries: bfloat16 [8, 8192, 1024], P('dp', 'ctx'), may hold values from -6 to 6
- keys: bfloat16 [8, 8192, 1024], P('dp', 'ctx'), may hold values from -6 to 6
- values: bfloat16 [8, 8192, 1024], P('dp', 'ctx'), may hold values from -6 to 6
- log_decay: float32 [8, 8, 8192], P('dp', None, 'ctx'), may hold values from -2 to 0
- gain: float32 [1024], replicated, may hold values from 0.1 to 1.9
- out_grad: bfloat16 [8, 8192, 1024], P('dp', 'ctx'), may hold values from -16 to 16
Outputs:
- query_grad: bfloat16 [8, 8192, 1024], P('dp', 'ctx')
- key_grad: bfloat16 [8, 8192, 1024], P('dp', 'ctx')
- value_grad: bfloat16 [8, 8192, 1024], P('dp', 'ctx')
- gain_grad: float32 [1024], P('ctx')
All inputs are finite; a program needn't handle non-finite values.
Results may differ from a plain program's by a relative error of at most 0.0059.
Values sent between devices are 32-bit elements; how exact they have to be, the bound alone decides.
A program may use at most 128 MiB of HBM per device.

v0:
```python
import jax
import jax.numpy as jnp
from jax import lax
from jax.sharding import PartitionSpec as P

EPSILON = 1e-06


def prefix(part, axis, combine, identity, reverse):
    count = lax.axis_size(axis)
    place = lax.axis_index(axis)
    ahead = count - 1 - place if reverse else place
    gathered = jax.tree.map(lambda a: lax.all_gather(a, axis), part)
    state = jax.tree.map(lambda a, e: jnp.zeros_like(a) + jnp.asarray(e, a.dtype), part, identity)

    def one(step, state):
        source = count - 1 - step if reverse else step
        return combine(
            state, jax.tree.map(lambda a: lax.dynamic_index_in_dim(a, source, 0, False), gathered)
        )

    return lax.fori_loop(0, ahead, one, state)


def combine(earlier, latter):
    earlier_decay, earlier_state = earlier
    latter_decay, latter_state = latter
    return (
        earlier_decay * latter_decay,
        latter_decay[..., None, None] * earlier_state + latter_state,
    )


def causal_decay(cumulative):
    length = cumulative.shape[-1]
    causal = jnp.tril(jnp.ones((length, length), dtype=bool))
    spread = cumulative[..., :, None] - cumulative[..., None, :]
    return jnp.where(causal, jnp.exp(jnp.where(causal, spread, 0.0)), 0.0)


def body(queries, keys, values, log_decay, gain, out_grad):
    batch_rows, length, full_width = queries.shape
    head_count = log_decay.shape[1]
    head_size = full_width // head_count
    query_heads = queries.reshape(batch_rows, length, head_count, head_size)
    key_heads = keys.reshape(batch_rows, length, head_count, head_size)
    value_heads = values.reshape(batch_rows, length, head_count, head_size)
    cumulative = jnp.cumsum(log_decay, axis=2)
    from_start = jnp.exp(cumulative).transpose(0, 2, 1)[..., None]
    to_end = jnp.exp(cumulative[..., -1:] - cumulative).transpose(0, 2, 1)[..., None]
    key_decayed = (key_heads * to_end).astype(jnp.bfloat16)
    block_state = jnp.einsum(
        "bthi,bthj->bhij", key_decayed, value_heads, preferred_element_type=jnp.float32
    )
    block_decay = jnp.exp(cumulative[..., -1])
    start_decay = jnp.ones_like(block_decay)
    start_state = jnp.zeros_like(block_state)
    entering = prefix(
        (block_decay, block_state), "ctx", combine, (start_decay, start_state), False
    )[1]
    entering_half = entering.astype(jnp.bfloat16)
    decay_mask = causal_decay(cumulative)
    scores = jnp.einsum(
        "bthi,bshi->bhts", query_heads, key_heads, preferred_element_type=jnp.float32
    )
    weights = (scores * decay_mask).astype(jnp.bfloat16)
    attended = from_start * jnp.einsum(
        "bthi,bhij->bthj", query_heads, entering_half, preferred_element_type=jnp.float32
    )
    attended = attended + jnp.einsum(
        "bhts,bshj->bthj", weights, value_heads, preferred_element_type=jnp.float32
    )
    root_mean = jnp.sqrt(jnp.mean(attended * attended, axis=-1, keepdims=True) + EPSILON)
    normed = attended / root_mean
    upstream = out_grad.reshape(batch_rows, length, head_count, head_size).astype(jnp.float32)
    scaled_up = gain.reshape(head_count, head_size) * upstream
    attended_grad = (
        (scaled_up - normed * jnp.mean(scaled_up * normed, axis=-1, keepdims=True)) / root_mean
    ).astype(jnp.bfloat16)
    gain_terms = jnp.sum(upstream * normed, axis=(0, 1)).reshape(full_width)
    portion = full_width // lax.axis_size("ctx")
    summed = lax.psum(gain_terms, ("dp", "ctx"))
    gain_grad = lax.dynamic_slice_in_dim(summed, lax.axis_index("ctx") * portion, portion)
    grad_scores = jnp.einsum(
        "bthj,bshj->bhts", attended_grad, value_heads, preferred_element_type=jnp.float32
    )
    grad_weights = (grad_scores * decay_mask).astype(jnp.bfloat16)
    query_grad = from_start * jnp.einsum(
        "bthj,bhij->bthi", attended_grad, entering_half, preferred_element_type=jnp.float32
    )
    query_grad = query_grad + jnp.einsum(
        "bhts,bshi->bthi", grad_weights, key_heads, preferred_element_type=jnp.float32
    )
    query_decayed = (query_heads * from_start).astype(jnp.bfloat16)
    block_adjoint = jnp.einsum(
        "bthi,bthj->bhij", query_decayed, attended_grad, preferred_element_type=jnp.float32
    )
    returned = prefix(
        (block_decay, block_adjoint), "ctx", combine, (start_decay, start_state), True
    )[1]
    returned_half = returned.astype(jnp.bfloat16)
    key_grad = to_end * jnp.einsum(
        "bthj,bhij->bthi", value_heads, returned_half, preferred_element_type=jnp.float32
    )
    key_grad = key_grad + jnp.einsum(
        "bhts,bthi->bshi", grad_weights, query_heads, preferred_element_type=jnp.float32
    )
    value_grad = to_end * jnp.einsum(
        "bthi,bhij->bthj", key_heads, returned_half, preferred_element_type=jnp.float32
    )
    value_grad = value_grad + jnp.einsum(
        "bhts,bthj->bshj", weights, attended_grad, preferred_element_type=jnp.float32
    )
    return (
        query_grad.reshape(batch_rows, length, full_width).astype(jnp.bfloat16),
        key_grad.reshape(batch_rows, length, full_width).astype(jnp.bfloat16),
        value_grad.reshape(batch_rows, length, full_width).astype(jnp.bfloat16),
        gain_grad,
    )


def solution(mesh):
    in_specs = (
        P("dp", "ctx", None),
        P("dp", "ctx", None),
        P("dp", "ctx", None),
        P("dp", None, "ctx"),
        P(),
        P("dp", "ctx", None),
    )
    out_specs = (P("dp", "ctx", None), P("dp", "ctx", None), P("dp", "ctx", None), P("ctx"))
    return jax.shard_map(body, mesh=mesh, in_specs=in_specs, out_specs=out_specs, check_vma=False)
```

profile of v0, /device:TPU:1, one launch (start us, length us, event | category | flops | bytes accessed | tf_op | source)
XLA Modules:
  0.0 764.6 jit_solution(14405945986678790667)
XLA Ops:
  11.9 71.4 %all-gather = f32[64,8,1]{1,2,0:T(1,128)S(1)} all-gather(f32[1,8,1]{1,2,0:T(1,128)S(1)} %copy.61), channel_id=2, replica_groups=mesh['dp'=8,'ctx'=64] {'ctx'}, dimensions={0}, use_global_device_ids=true | all-gather | bytes 2080 | tf_op jit(solution)/shard_map/all_gather | solution.py:13
  86.4 224.8 %all-gather.6.cloned.1.call-done = f32[512,128,128]{2,1,0:T(8,128)} async-done(((f32[8,128,128]{2,1,0:T(8,128)}), f32[512,128,128]{2,1,0:T(8,128)}) %all-gather.6.cloned.1.call-update) | async-done | bytes 33554448 | tf_op jit(solution)/shard_map/all_gather | solution.py:13
  316.4 177.8 %psum.7 = f32[1024]{0:T(1024)S(1)} all-reduce(f32[1024]{0:T(1024)S(1)} %bitcast.158), channel_id=1, replica_groups=mesh['dp'=8,'ctx'=64] {'dp','ctx'}, use_global_device_ids=true, to_apply=%region_8.9 | all-reduce | flops 1024 | bytes 8192 | tf_op jit(solution)/shard_map/psum | solution.py:82
  495.2 182.3 %all-gather.8.cloned.1.call-done = f32[512,128,128]{2,1,0:T(8,128)} async-done(((f32[8,128,128]{2,1,0:T(8,128)}), f32[512,128,128]{2,1,0:T(8,128)}) %all-gather.8.cloned.1.call-update) | async-done | bytes 33554448 | tf_op jit(solution)/shard_map/all_gather | solution.py:13
  677.6 77.8 %while.27 = (s32[]{:T(128)}, f32[1,8,128,128]{3,2,1,0:T(8,128)S(1)}, s32[]{:T(128)}, f32[64,1,8]{2,1,0:T(1,128)S(1)}, f32[64,1,8,128,128]{4,3,2,1,0:T(8,128)}, /*index=5*/s32[]{:T(128)}, s32[]{:T(128)}, s32[]{:T(128)}, s32[]{:T(128)}) while((s32[]{:T(128)}, f32[1,8,128,128]{3,2,1,0:T(8,128)S(1)}, s32[]{:T(128)}, f32[64,1,8]{2,1,0:T(1,128)S(1)}, ...), condition=%wide.region_6.7_spmd, body=%wide.region_5.6_spmd.sunk | while | flops 262150 | bytes 1573107 | solution.py:22
  677.6 1.2 bitcast_add_fusion.5
  678.8 1.2 bitcast_add_fusion.5
  680.1 1.2 bitcast_add_fusion.5
  681.3 1.2 bitcast_add_fusion.5
  682.5 1.2 bitcast_add_fusion.5
  683.8 1.2 bitcast_add_fusion.5
  685.0 1.2 bitcast_add_fusion.5
  686.2 1.2 bitcast_add_fusion.5
  687.5 1.2 bitcast_add_fusion.5
  688.7 1.2 bitcast_add_fusion.5
  689.9 1.2 bitcast_add_fusion.5
  693.6 1.2 bitcast_add_fusion.5
  694.9 1.2 bitcast_add_fusion.5
  696.1 1.2 bitcast_add_fusion.5
  697.4 1.2 bitcast_add_fusion.5
  701.1 1.2 bitcast_add_fusion.5
  702.3 1.2 bitcast_add_fusion.5
  703.5 1.2 bitcast_add_fusion.5
  704.8 1.2 bitcast_add_fusion.5
  709.7 1.2 bitcast_add_fusion.5
  710.9 1.2 bitcast_add_fusion.5
  712.2 1.2 bitcast_add_fusion.5
  713.4 1.2 bitcast_add_fusion.5
  717.1 1.2 bitcast_add_fusion.5
  718.3 1.2 bitcast_add_fusion.5
  719.6 1.2 bitcast_add_fusion.5
  720.8 1.2 bitcast_add_fusion.5
  724.5 1.2 bitcast_add_fusion.5
  725.8 1.2 bitcast_add_fusion.5
  727.0 1.2 bitcast_add_fusion.5
  728.2 1.2 bitcast_add_fusion.5
  733.2 1.2 bitcast_add_fusion.5
  734.4 1.2 bitcast_add_fusion.5
  735.6 1.2 bitcast_add_fusion.5
  736.9 1.2 bitcast_add_fusion.5
  740.6 1.2 bitcast_add_fusion.5
  741.8 1.2 bitcast_add_fusion.5
  743.0 1.2 bitcast_add_fusion.5
  744.3 1.2 bitcast_add_fusion.5
  748.0 1.2 bitcast_add_fusion.5
  749.2 1.2 bitcast_add_fusion.5
  750.4 1.2 bitcast_add_fusion.5
  751.7 1.2 bitcast_add_fusion.5
  (122 shorter events, 40.5 us)
Async XLA Ops:
  7.2 304.0 %all-gather.6.cloned.1.call-start = ((), (), s32[]{:S(2)}) async-start(), calls=%async_computation | async-start | bytes 34078720 | tf_op jit(solution)/shard_map/all_gather | solution.py:13
  11.7 665.8 %all-gather.8.cloned.1.call-start = ((), (), s32[]{:S(2)}) async-start(), calls=%async_computation.1 | async-start | bytes 34078720 | tf_op jit(solution)/shard_map/all_gather | solution.py:13
Sparse Core Ops, SparseCore 0:
  11.8 299.2 all-gather.5
  314.8 362.6 all-gather.7
where the time goes:
time: 768 us; the launch traced here: 765 us
  waiting for transfers between devices  407 us (53%)
  blocking collectives  249 us (32%)
  other arithmetic  78 us (10%)
  between operations  14.2 us (2%)
  local copies, waits for them, and re-layouts  8.53 us (1%)
    all_gather x2, waiting for transfers between devices, prefix(): gathered = jax.tree.map(lambda a: lax.all_gather(a, axis), part)  407 us
    psum x1, blocking collectives, body(): summed = lax.psum(gain_terms, ('dp', 'ctx'))  178 us
    add x63, other arithmetic, combine(): latter_decay[..., None, None] * earlier_state + latter_state  75 us
    all_gather x1, blocking collectives, prefix(): gathered = jax.tree.map(lambda a: lax.all_gather(a, axis), part)  71.4 us
  transfers between devices with their start and end apart: 2, of which 2 were waited for; matrix products, arithmetic and copies ran while one was open for 1% of the time, Pallas kernels for 0%

commit v1 on v0

--- a/solution.py
+++ b/solution.py
@@ -79,7 +79,7 @@
     ).astype(jnp.bfloat16)
     gain_terms = jnp.sum(upstream * normed, axis=(0, 1)).reshape(full_width)
     portion = full_width // lax.axis_size("ctx")
-    summed = lax.psum(gain_terms, ("dp", "ctx"))
+    summed = jnp.sum(lax.all_gather(gain_terms, ("dp", "ctx")), axis=0)
     gain_grad = lax.dynamic_slice_in_dim(summed, lax.axis_index("ctx") * portion, portion)
     grad_scores = jnp.einsum(
         "bthj,bshj->bhts", attended_grad, value_heads, preferred_element_type=jnp.float32

time: 768 us -> 958 us (1.25)
  waiting for transfers between devices: 407 us -> 772 us
  blocking collectives: 249 us -> 71.4 us
    all_gather x0 -> x1, waiting for transfers between devices: none -> 258 us  [body(): summed = jnp.sum(lax.all_gather(gain_terms, ('dp', 'ctx')), axis=0)]
    psum x1 -> x0, blocking collectives: 178 us -> none  [body(): summed = lax.psum(gain_terms, ('dp', 'ctx'))]
    all_gather x2, waiting for transfers between devices: 407 us -> 514 us  [prefix(): gathered = jax.tree.map(lambda a: lax.all_gather(a, axis), part)]
  transfers between devices with their start and end apart: 2 -> 3, of which waited for: 2 -> 3; matrix products, arithmetic and copies ran while one was open for 1% -> 1% of each run, Pallas kernels for 0% -> 0%
where the time goes in v1:
time: 958 us; the launch traced here: 954 us
  waiting for transfers between devices  772 us (81%)
  other arithmetic  81.4 us (8%)
  blocking collectives  71.4 us (7%)
  between operations  13.9 us (1%)
    all_gather x2, waiting for transfers between devices, prefix(): gathered = jax.tree.map(lambda a: lax.all_gather(a, axis), part)  514 us
    all_gather x1, waiting for transfers between devices, body(): summed = jnp.sum(lax.all_gather(gain_terms, ('dp', 'ctx')), axis=0)  258 us
    add x63, other arithmetic, combine(): latter_decay[..., None, None] * earlier_state + latter_state  75 us
    all_gather x1, blocking collectives, prefix(): gathered = jax.tree.map(lambda a: lax.all_gather(a, axis), part)  71.4 us
  transfers between devices with their start and end apart: 3, of which 3 were waited for; matrix products, arithmetic and copies ran while one was open for 1% of the time, Pallas kernels for 0%

profile of v1, /device:TPU:1, one launch (start us, length us, event | category | flops | bytes accessed | tf_op | source)
XLA Modules:
  0.0 954.3 jit_solution(3904094104519826624)
XLA Ops:
  11.9 71.4 %all-gather = f32[64,8,1]{1,2,0:T(1,128)S(1)} all-gather(f32[1,8,1]{1,2,0:T(1,128)S(1)} %copy.61), channel_id=2, replica_groups=mesh['dp'=8,'ctx'=64] {'ctx'}, dimensions={0}, use_global_device_ids=true | all-gather | bytes 2080 | tf_op jit(solution)/shard_map/all_gather | solution.py:13
  86.4 224.8 %all-gather.8.cloned.1.call-done = f32[512,128,128]{2,1,0:T(8,128)} async-done(((f32[8,128,128]{2,1,0:T(8,128)}), f32[512,128,128]{2,1,0:T(8,128)}) %all-gather.8.cloned.1.call-update) | async-done | bytes 33554448 | tf_op jit(solution)/shard_map/all_gather | solution.py:13
  311.6 1.6 multiply_reduce_fusion
  317.5 257.8 %all-gather.12.cloned.1.call-done = f32[512,1,1024]{2,1,0:T(1,128)} async-done(((f32[1,1,1024]{2,1,0:T(1,128)}), f32[512,1,1024]{2,1,0:T(1,128)}) %all-gather.12.cloned.1.call-update) | async-done | bytes 2097168 | tf_op jit(solution)/shard_map/all_gather | solution.py:82
  575.3 2.8 reduce_sum.39
  578.7 288.9 %all-gather.10.cloned.1.call-done = f32[512,128,128]{2,1,0:T(8,128)} async-done(((f32[8,128,128]{2,1,0:T(8,128)}), f32[512,128,128]{2,1,0:T(8,128)}) %all-gather.10.cloned.1.call-update) | async-done | bytes 33554448 | tf_op jit(solution)/shard_map/all_gather | solution.py:13
  867.6 77.8 %while.27 = (s32[]{:T(128)}, f32[1,8,128,128]{3,2,1,0:T(8,128)S(1)}, s32[]{:T(128)}, f32[64,1,8]{2,1,0:T(1,128)S(1)}, f32[64,1,8,128,128]{4,3,2,1,0:T(8,128)}, /*index=5*/s32[]{:T(128)}, s32[]{:T(128)}, s32[]{:T(128)}, s32[]{:T(128)}) while((s32[]{:T(128)}, f32[1,8,128,128]{3,2,1,0:T(8,128)S(1)}, s32[]{:T(128)}, f32[64,1,8]{2,1,0:T(1,128)S(1)}, ...), condition=%wide.region_6.7_spmd, body=%wide.region_5.6_spmd.sunk | while | flops 262150 | bytes 1573107 | solution.py:22
  867.6 1.2 bitcast_add_fusion.5
  868.9 1.2 bitcast_add_fusion.5
  870.1 1.2 bitcast_add_fusion.5
  871.3 1.2 bitcast_add_fusion.5
  872.6 1.2 bitcast_add_fusion.5
  877.5 1.2 bitcast_add_fusion.5
  878.8 1.2 bitcast_add_fusion.5
  880.0 1.2 bitcast_add_fusion.5
  881.2 1.2 bitcast_add_fusion.5
  884.9 1.2 bitcast_add_fusion.5
  886.2 1.2 bitcast_add_fusion.5
  887.4 1.2 bitcast_add_fusion.5
  888.6 1.2 bitcast_add_fusion.5
  892.3 1.2 bitcast_add_fusion.5
  893.6 1.2 bitcast_add_fusion.5
  894.8 1.2 bitcast_add_fusion.5
  896.0 1.2 bitcast_add_fusion.5
  901.0 1.2 bitcast_add_fusion.5
  902.2 1.2 bitcast_add_fusion.5
  903.4 1.2 bitcast_add_fusion.5
  904.7 1.2 bitcast_add_fusion.5
  908.4 1.2 bitcast_add_fusion.5
  909.6 1.2 bitcast_add_fusion.5
  910.9 1.2 bitcast_add_fusion.5
  912.1 1.2 bitcast_add_fusion.5
  915.8 1.2 bitcast_add_fusion.5
  917.0 1.2 bitcast_add_fusion.5
  918.3 1.2 bitcast_add_fusion.5
  919.5 1.2 bitcast_add_fusion.5
  924.4 1.2 bitcast_add_fusion.5
  925.7 1.2 bitcast_add_fusion.5
  926.9 1.2 bitcast_add_fusion.5
  928.1 1.2 bitcast_add_fusion.5
  931.8 1.2 bitcast_add_fusion.5
  933.1 1.2 bitcast_add_fusion.5
  934.3 1.2 bitcast_add_fusion.5
  935.6 1.2 bitcast_add_fusion.5
  939.3 1.2 bitcast_add_fusion.5
  940.5 1.2 bitcast_add_fusion.5
  941.7 1.2 bitcast_add_fusion.5
  943.0 1.2 bitcast_add_fusion.5
  (125 shorter events, 41.9 us)
Async XLA Ops:
  7.2 304.0 %all-gather.8.cloned.1.call-start = ((), (), s32[]{:S(2)}) async-start(), calls=%async_computation | async-start | bytes 34078720 | tf_op jit(solution)/shard_map/all_gather | solution.py:13
  11.7 563.6 %all-gather.12.cloned.1.call-start = ((), (), s32[]{:S(2)}) async-start(), calls=%async_computation.2 | async-start | bytes 2101248 | tf_op jit(solution)/shard_map/all_gather | solution.py:82
  313.2 554.3 %all-gather.10.cloned.1.call-start = ((), (), s32[]{:S(2)}) async-start(), calls=%async_computation.1 | async-start | bytes 34078720 | tf_op jit(solution)/shard_map/all_gather | solution.py:13
Sparse Core Ops, SparseCore 0:
  11.8 299.2 all-gather.7
  316.4 258.9 all-gather.11
  578.3 289.2 all-gather.9
